TPU v7x, 512 devices: a whole 4x8x8 slice. The times are simulated.
512 devices in a mesh: seq: 64 (over y, x, core), head: 8 (over z).
Axes of the slice: x: 4, y: 8, z: 8, core: 2. Of those that a mesh axis runs over, the one named last changes fastest.
Arguments:
- token_values: bfloat16 [24576, 4096], P('seq', 'head'), may hold values from -6 to 6
- b_inputs: bfloat16 [24576, 128], P('seq'), may hold values from -6 to 6
- c_inputs: bfloat16 [24576, 128], P('seq'), may hold values from -6 to 6
- log_decay: float32 [64, 24576], P('head', 'seq'), may hold values from -1 to 0
- grad_out: bfloat16 [24576, 4096], P('seq', 'head'), may hold values from -0.005859375 to 0.005859375
Outputs:
- grad_values: bfloat16 [24576, 4096], P('seq', 'head')
- grad_b: bfloat16 [24576, 128], P('seq')
- grad_c: bfloat16 [24576, 128], P('seq')
All inputs are finite; a program needn't handle non-finite values.
Results may differ from a plain program's by a relative error of at most 0.014.
Values may be sent and summed in bfloat16 or wider, within the bound.
A program may use at most 128 MiB of HBM per device.

v0:
```python
import functools
import jax
import jax.numpy as jnp
from jax import lax
from jax.sharding import PartitionSpec as P

PRECISE = lax.Precision.HIGHEST


def shift(value, count, distance, reverse):
    if reverse:
        pairs = [(p, p - distance) for p in range(distance, count)]
    else:
        pairs = [(p, p + distance) for p in range(count - distance)]
    return lax.ppermute(value, "seq", pairs)


def exclusive_scans(count, decay_cols, parts):
    packed = [jnp.concatenate([decay_cols, s], axis=0) for s, _ in parts]
    windows = [shift(pk, count, 1, rev) for pk, (_, rev) in zip(packed, parts)]
    distance = 1
    while distance < count:
        received = [shift(w, count, distance, rev) for w, (_, rev) in zip(windows, parts)]
        windows = [
            jnp.concatenate([w[:1] * r[:1], w[1:] + w[:1] * r[1:]], axis=0)
            for w, r in zip(windows, received)
        ]
        distance *= 2
    return [w[1:] for w in windows]


def shards(count, token_values, b_inputs, c_inputs, log_decay, grad_out):
    length = token_values.shape[0]
    heads_here = log_decay.shape[0]
    head_dim = token_values.shape[1] // heads_here
    state_size = b_inputs.shape[1]
    cumulative = jnp.cumsum(log_decay, axis=1)
    block_log = cumulative[:, -1]
    into_end = jnp.exp(block_log[:, None] - cumulative)
    from_start = jnp.exp(cumulative)
    block_decay = jnp.exp(block_log)
    b_float = b_inputs.astype(jnp.float32)
    c_float = c_inputs.astype(jnp.float32)
    decayed_b = (into_end[:, :, None] * b_float[None]).astype(jnp.bfloat16)
    decayed_c = (from_start[:, :, None] * c_float[None]).astype(jnp.bfloat16)
    x_heads = token_values.reshape(length, heads_here, head_dim)
    dy_heads = grad_out.reshape(length, heads_here, head_dim)
    state_local = jnp.einsum(
        "htn,thp->nhp", decayed_b, x_heads, preferred_element_type=jnp.float32
    ).reshape(state_size, heads_here * head_dim)
    adjoint_local = jnp.einsum(
        "hsn,shp->nhp", decayed_c, dy_heads, preferred_element_type=jnp.float32
    ).reshape(state_size, heads_here * head_dim)
    decay_cols = jnp.repeat(block_decay, head_dim)[None, :]
    state_in, adjoint_out = exclusive_scans(
        count, decay_cols, [(state_local, False), (adjoint_local, True)]
    )
    scores = lax.dot_general(
        c_inputs, b_inputs, (((1,), (1,)), ((), ())), preferred_element_type=jnp.float32
    )
    entry_indices = lax.iota(jnp.int32, length)
    causal = entry_indices[:, None] >= entry_indices[None, :]

    def head_step(head_idx, carried):
        running, dx_local = carried
        cum_head = lax.dynamic_index_in_dim(cumulative, head_idx, 0, keepdims=False)
        log_gaps = cum_head[:, None] - cum_head[None, :]
        decays = jnp.where(causal, jnp.exp(jnp.where(causal, log_gaps, 0.0)), 0.0)
        mixing = (scores * decays).astype(jnp.bfloat16)
        x_head = lax.dynamic_slice_in_dim(token_values, head_idx * head_dim, head_dim, 1)
        dy_head = lax.dynamic_slice_in_dim(grad_out, head_idx * head_dim, head_dim, 1)
        dx_head = lax.dot_general(
            mixing, dy_head, (((0,), (0,)), ((), ())), preferred_element_type=jnp.float32
        )
        dot_pairs = lax.dot_general(
            dy_head, x_head, (((1,), (1,)), ((), ())), preferred_element_type=jnp.float32
        )
        dx_local = lax.dynamic_update_slice_in_dim(dx_local, dx_head, head_idx * head_dim, 1)
        return (running + decays * dot_pairs, dx_local)

    start_pair = (
        jnp.zeros((length, length), jnp.float32),
        jnp.zeros((length, heads_here * head_dim), jnp.float32),
    )
    running, dx_local = lax.fori_loop(0, heads_here, head_step, start_pair)
    weighted = running.astype(jnp.bfloat16)
    db_part = lax.dot_general(
        weighted, c_inputs, (((0,), (0,)), ((), ())), preferred_element_type=jnp.float32
    )
    dc_part = jnp.dot(weighted, b_inputs, preferred_element_type=jnp.float32)
    to_end_cols = jnp.repeat(into_end.T, head_dim, axis=1)
    from_start_cols = jnp.repeat(from_start.T, head_dim, axis=1)
    grad_values = dx_local + to_end_cols * jnp.dot(b_float, adjoint_out, precision=PRECISE)
    db_part = db_part + jnp.dot(
        token_values.astype(jnp.float32) * to_end_cols, adjoint_out.T, precision=PRECISE
    )
    dc_part = dc_part + jnp.dot(
        grad_out.astype(jnp.float32) * from_start_cols, state_in.T, precision=PRECISE
    )
    grad_b, grad_c = (
        lax.psum(db_part.astype(jnp.bfloat16), "head").astype(jnp.float32),
        lax.psum(dc_part.astype(jnp.bfloat16), "head").astype(jnp.float32),
    )
    return (
        grad_values.astype(jnp.bfloat16),
        grad_b.astype(jnp.bfloat16),
        grad_c.astype(jnp.bfloat16),
    )


def solution(mesh):
    in_specs = (
        P("seq", "head"),
        P("seq", None),
        P("seq", None),
        P("head", "seq"),
        P("seq", "head"),
    )
    out_specs = (P("seq", "head"), P("seq", None), P("seq", None))
    body = functools.partial(shards, mesh.shape["seq"])
    return jax.shard_map(body, mesh=mesh, in_specs=in_specs, out_specs=out_specs, check_vma=False)
```

profile of v0, /device:TPU:2, one launch (start us, length us, event | category | flops | bytes accessed | tf_op | source)
XLA Modules:
  0.0 233.3 jit_solution(7088750057124576250)
XLA Ops:
  7.2 1.9 reduce-window.6
  9.2 0.2 slice_reduce_fusion
  9.4 0.2 slice_reduce_fusion.1
  9.8 1.2 copy.15
  11.1 0.6 fusion.21
  11.9 0.2 copy-done.2
  12.1 0.2 copy.13
  12.3 0.3 copy-done.1
  12.7 0.6 fusion.20
  13.4 0.8 pad_maximum_fusion
  14.2 1.9 collective-permute-start
  16.1 2.4 %collective-permute-start.7 = (f32[129,512]{1,0:T(8,128)S(1)}, f32[129,512]{1,0:T(8,128)}, u32[]{:S(2)}, u32[]{:S(2)}) collective-permute-start(f32[129,512]{1,0:T(8,128)S(1)} %get-tuple-element.224), channel_id=1, source_target_pairs={{0,8},{8,16},{16,24},{24,32},{32,40},{40,48},{48,56},{56,64},{64,7... | collective-permute-start | bytes 792584 | tf_op jit(solution)/shard_map/ppermute | solution.py:15
  18.6 0.3 fusion.47
  18.9 21.5 %while.17 = (s32[]{:T(128)}, f32[384,384]{1,0:T(8,128)S(1)}, f32[384,512]{0,1:T(8,128)S(1)}, f32[8,384]{1,0:T(8,128)S(1)}, bf16[384,512]{1,0:T(8,128)(2,1)}, /*i...) while((s32[]{:T(128)}, f32[384,384]{1,0:T(8,128)S(1)}, ...), condition=%wide.region_3.4_spmd.clone.clone, body=%wide.region_2.3_spmd.clone.clone.sunk | while | flops 39665672 | bytes 2176688 | solution.py:85
  18.9 1.4 fusion.64
  20.3 1.2 convolution_dynamic-update-slice_fusion.2
  21.6 1.4 fusion.64
  23.0 1.2 convolution_dynamic-update-slice_fusion.2
  24.3 1.4 fusion.64
  25.7 1.2 convolution_dynamic-update-slice_fusion.2
  27.0 1.4 fusion.64
  28.4 1.2 convolution_dynamic-update-slice_fusion.2
  29.7 1.4 fusion.64
  31.1 1.2 convolution_dynamic-update-slice_fusion.2
  32.3 1.4 fusion.64
  33.7 1.2 convolution_dynamic-update-slice_fusion.2
  35.0 1.4 fusion.64
  36.4 1.2 convolution_dynamic-update-slice_fusion.2
  37.7 1.4 fusion.64
  39.1 1.2 convolution_dynamic-update-slice_fusion.2
  40.4 7.4 %collective-permute-start.1 = (f32[129,512]{1,0:T(8,128)}, f32[129,512]{1,0:T(8,128)S(1)}, u32[]{:S(2)}, u32[]{:S(2)}) collective-permute-start(f32[129,512]{1,0:T(8,128)} %collective-permute-done), channel_id=1, source_target_pairs={{8,0},{16,8},{24,16},{32,24},{40,32},{48,40},{56,48},{64,56},{72,6... | collective-permute-start | bytes 792584 | tf_op jit(solution)/shard_map/ppermute | solution.py:15
  47.8 0.3 fusion.41
  48.2 0.2 fusion.39
  48.5 1.9 collective-permute-start.8
  50.4 1.8 collective-permute-done.1
  52.2 0.7 slice_multiply_fusion.21
  52.9 1.0 fusion.38
  53.9 1.9 collective-permute-start.2
  55.9 0.7 collective-permute-done.8
  56.5 0.7 slice_multiply_fusion.16
  57.3 1.0 fusion.32
  58.3 3.3 %collective-permute-start.9 = (f32[129,512]{1,0:T(8,128)S(1)}, f32[129,512]{1,0:T(8,128)S(1)}, u32[]{:S(2)}, u32[]{:S(2)}) collective-permute-start(f32[129,512]{1,0:T(8,128)S(1)} %pad_maximum_fusion.7), channel_id=1, source_target_pairs={{0,16},{8,24},{16,32},{24,40},{32,48},{40,56},{48,64},{56,72},{64,... | collective-permute-start | bytes 792584 | tf_op jit(solution)/shard_map/ppermute | solution.py:15
  61.6 0.8 collective-permute-done.2
  62.5 1.3 collective-permute-start.3
  63.8 11.6 %collective-permute-done.9 = f32[129,512]{1,0:T(8,128)S(1)} collective-permute-done((f32[129,512]{1,0:T(8,128)S(1)}, f32[129,512]{1,0:T(8,128)S(1)}, u32[]{:S(2)}, u32[]{:S(2)}) %collective-permute-start.9) | collective-permute-done | bytes 264224 | tf_op jit(solution)/shard_map/ppermute | solution.py:15
  75.5 2.3 collective-permute-start.10
  78.0 1.3 collective-permute-start.4
  79.3 5.3 %collective-permute-done.10 = f32[129,512]{1,0:T(8,128)S(1)} collective-permute-done((f32[129,512]{1,0:T(8,128)S(1)}, f32[129,512]{1,0:T(8,128)S(1)}, u32[]{:S(2)}, u32[]{:S(2)}) %collective-permute-start.10) | collective-permute-done | bytes 264224 | tf_op jit(solution)/shard_map/ppermute | solution.py:15
  84.7 7.9 %collective-permute-start.11 = (f32[129,512]{1,0:T(8,128)S(1)}, f32[129,512]{1,0:T(8,128)S(1)}, u32[]{:S(2)}, u32[]{:S(2)}) collective-permute-start(f32[129,512]{1,0:T(8,128)S(1)} %pad_maximum_fusion.9), channel_id=1, source_target_pairs={{0,64},{8,72},{16,80},{24,88},{32,96},{40,104},{48,112},{56,120},{... | collective-permute-start | bytes 792584 | tf_op jit(solution)/shard_map/ppermute | solution.py:15
  92.7 1.3 collective-permute-start.5
  94.0 4.1 %collective-permute-done.11 = f32[129,512]{1,0:T(8,128)S(1)} collective-permute-done((f32[129,512]{1,0:T(8,128)S(1)}, f32[129,512]{1,0:T(8,128)S(1)}, u32[]{:S(2)}, u32[]{:S(2)}) %collective-permute-start.11) | collective-permute-done | bytes 264224 | tf_op jit(solution)/shard_map/ppermute | solution.py:15
  98.3 5.4 %collective-permute-start.12 = (f32[129,512]{1,0:T(8,128)S(1)}, f32[129,512]{1,0:T(8,128)S(1)}, u32[]{:S(2)}, u32[]{:S(2)}) collective-permute-start(f32[129,512]{1,0:T(8,128)S(1)} %pad_maximum_fusion.10), channel_id=1, source_target_pairs={{0,128},{8,136},{16,144},{24,152},{32,160},{40,168},{48,176},{56,1... | collective-permute-start | bytes 792584 | tf_op jit(solution)/shard_map/ppermute | solution.py:15
  103.7 5.6 %collective-permute-done.5 = f32[129,512]{1,0:T(8,128)S(1)} collective-permute-done((f32[129,512]{1,0:T(8,128)S(1)}, f32[129,512]{1,0:T(8,128)S(1)}, u32[]{:S(2)}, u32[]{:S(2)}) %collective-permute-start.5) | collective-permute-done | bytes 264224 | tf_op jit(solution)/shard_map/ppermute | solution.py:15
  109.4 1.3 collective-permute-start.6
  110.8 17.8 %collective-permute-start.13 = (f32[129,512]{1,0:T(8,128)S(1)}, f32[129,512]{1,0:T(8,128)S(1)}, u32[]{:S(2)}, u32[]{:S(2)}) collective-permute-start(f32[129,512]{1,0:T(8,128)S(1)} %pad_maximum_fusion.11), channel_id=1, source_target_pairs={{0,256},{8,264},{16,272},{24,280},{32,288},{40,296},{48,304},{56,3... | collective-permute-start | bytes 792584 | tf_op jit(solution)/shard_map/ppermute | solution.py:15
  128.7 0.5 collective-permute-done.6
  129.2 2.1 fusion.18
  131.3 3.5 %collective-permute-done.13 = f32[129,512]{1,0:T(8,128)S(1)} collective-permute-done((f32[129,512]{1,0:T(8,128)S(1)}, f32[129,512]{1,0:T(8,128)S(1)}, u32[]{:S(2)}, u32[]{:S(2)}) %collective-permute-start.13) | collective-permute-done | bytes 264224 | tf_op jit(solution)/shard_map/ppermute | solution.py:15
  134.7 2.1 fusion.19
  136.9 0.7 fusion.17
  137.6 0.9 copy.19
  138.5 84.9 %all-reduce.3.cloned.1.call-done = (bf16[384,128]{1,0:T(8,128)(2,1)}, bf16[384,128]{1,0:T(8,128)(2,1)}) async-done(((bf16[384,128]{1,0:T(8,128)(2,1)}, bf16[384,128]{1,0:T(8,128)(2,1)}), (bf16[384,128]{1,0:T(8,128)(2,1)}, bf16[384,128]{1,0:T(8,128)(2,1)})) %all-reduce.3.cloned.1.call-update) | async-done | bytes 196624 | tf_op jit(solution)/shard_map/psum | solution.py:101
  223.4 1.5 copy.32
  224.9 1.5 copy.33
  (60 shorter events, 1.8 us)
Async XLA Ops:
  7.2 3.9 %copy-start = (bf16[384,128]{1,0:T(8,128)(2,1)S(1)}, bf16[384,128]{1,0:T(8,128)(2,1)}, u32[]{:S(2)}) copy-start(bf16[384,128]{1,0:T(8,128)(2,1)} %param.8) | copy-start | bytes 294916
  7.2 216.2 %all-reduce.3.cloned.1.call-start = ((), (), s32[]{:S(2)}) async-start(), calls=%async_computation | async-start | bytes 393216 | tf_op jit(solution)/shard_map/psum | solution.py:101
  11.1 1.0 copy-start.2
  11.7 0.9 copy-start.1
  14.2 26.1 %collective-permute-start = (f32[129,512]{1,0:T(8,128)}, f32[129,512]{1,0:T(8,128)}, u32[]{:S(2)}, u32[]{:S(2)}) collective-permute-start(f32[129,512]{1,0:T(8,128)} %get-tuple-element.225), channel_id=1, source_target_pairs={{8,0},{16,8},{24,16},{32,24},{40,32},{48,40},{56,48},{64,56},{72,6... | collective-permute-start | bytes 792584 | tf_op jit(solution)/shard_map/ppermute | solution.py:15
  16.1 32.3 %collective-permute-start.7 = (f32[129,512]{1,0:T(8,128)S(1)}, f32[129,512]{1,0:T(8,128)}, u32[]{:S(2)}, u32[]{:S(2)}) collective-permute-start(f32[129,512]{1,0:T(8,128)S(1)} %get-tuple-element.224), channel_id=1, source_target_pairs={{0,8},{8,16},{16,24},{24,32},{32,40},{40,48},{48,56},{56,64},{64,7... | collective-permute-start | bytes 792584 | tf_op jit(solution)/shard_map/ppermute | solution.py:15
  40.4 11.8 %collective-permute-start.1 = (f32[129,512]{1,0:T(8,128)}, f32[129,512]{1,0:T(8,128)S(1)}, u32[]{:S(2)}, u32[]{:S(2)}) collective-permute-start(f32[129,512]{1,0:T(8,128)} %collective-permute-done), channel_id=1, source_target_pairs={{8,0},{16,8},{24,16},{32,24},{40,32},{48,40},{56,48},{64,56},{72,6... | collective-permute-start | bytes 792584 | tf_op jit(solution)/shard_map/ppermute | solution.py:15
  48.5 8.1 %collective-permute-start.8 = (f32[129,512]{1,0:T(8,128)}, f32[129,512]{1,0:T(8,128)S(1)}, u32[]{:S(2)}, u32[]{:S(2)}) collective-permute-start(f32[129,512]{1,0:T(8,128)} %collective-permute-done.7), channel_id=1, source_target_pairs={{0,8},{8,16},{16,24},{24,32},{32,40},{40,48},{48,56},{56,64},{64,7... | collective-permute-start | bytes 792584 | tf_op jit(solution)/shard_map/ppermute | solution.py:15
  53.9 8.4 %collective-permute-start.2 = (f32[129,512]{1,0:T(8,128)S(1)}, f32[129,512]{1,0:T(8,128)S(1)}, u32[]{:S(2)}, u32[]{:S(2)}) collective-permute-start(f32[129,512]{1,0:T(8,128)S(1)} %pad_maximum_fusion.2), channel_id=1, source_target_pairs={{16,0},{24,8},{32,16},{40,24},{48,32},{56,40},{64,48},{72,56},{80,... | collective-permute-start | bytes 792584 | tf_op jit(solution)/shard_map/ppermute | solution.py:15
  58.3 17.1 %collective-permute-start.9 = (f32[129,512]{1,0:T(8,128)S(1)}, f32[129,512]{1,0:T(8,128)S(1)}, u32[]{:S(2)}, u32[]{:S(2)}) collective-permute-start(f32[129,512]{1,0:T(8,128)S(1)} %pad_maximum_fusion.7), channel_id=1, source_target_pairs={{0,16},{8,24},{16,32},{24,40},{32,48},{40,56},{48,64},{56,72},{64,... | collective-permute-start | bytes 792584 | tf_op jit(solution)/shard_map/ppermute | solution.py:15
  62.5 15.4 %collective-permute-start.3 = (f32[129,512]{1,0:T(8,128)S(1)}, f32[129,512]{1,0:T(8,128)S(1)}, u32[]{:S(2)}, u32[]{:S(2)}) collective-permute-start(f32[129,512]{1,0:T(8,128)S(1)} %pad_maximum_fusion.3), channel_id=1, source_target_pairs={{32,0},{40,8},{48,16},{56,24},{64,32},{72,40},{80,48},{88,56},{96,... | collective-permute-start | bytes 792584 | tf_op jit(solution)/shard_map/ppermute | solution.py:15
  75.5 9.1 %collective-permute-start.10 = (f32[129,512]{1,0:T(8,128)S(1)}, f32[129,512]{1,0:T(8,128)S(1)}, u32[]{:S(2)}, u32[]{:S(2)}) collective-permute-start(f32[129,512]{1,0:T(8,128)S(1)} %pad_maximum_fusion.8), channel_id=1, source_target_pairs={{0,32},{8,40},{16,48},{24,56},{32,64},{40,72},{48,80},{56,88},{64,... | collective-permute-start | bytes 792584 | tf_op jit(solution)/shard_map/ppermute | solution.py:15
  78.0 14.7 %collective-permute-start.4 = (f32[129,512]{1,0:T(8,128)S(1)}, f32[129,512]{1,0:T(8,128)S(1)}, u32[]{:S(2)}, u32[]{:S(2)}) collective-permute-start(f32[129,512]{1,0:T(8,128)S(1)} %pad_maximum_fusion.4), channel_id=1, source_target_pairs={{64,0},{72,8},{80,16},{88,24},{96,32},{104,40},{112,48},{120,56},{... | collective-permute-start | bytes 792584 | tf_op jit(solution)/shard_map/ppermute | solution.py:15
  84.7 13.5 %collective-permute-start.11 = (f32[129,512]{1,0:T(8,128)S(1)}, f32[129,512]{1,0:T(8,128)S(1)}, u32[]{:S(2)}, u32[]{:S(2)}) collective-permute-start(f32[129,512]{1,0:T(8,128)S(1)} %pad_maximum_fusion.9), channel_id=1, source_target_pairs={{0,64},{8,72},{16,80},{24,88},{32,96},{40,104},{48,112},{56,120},{... | collective-permute-start | bytes 792584 | tf_op jit(solution)/shard_map/ppermute | solution.py:15
  92.7 16.6 %collective-permute-start.5 = (f32[129,512]{1,0:T(8,128)S(1)}, f32[129,512]{1,0:T(8,128)S(1)}, u32[]{:S(2)}, u32[]{:S(2)}) collective-permute-start(f32[129,512]{1,0:T(8,128)S(1)} %pad_maximum_fusion.5), channel_id=1, source_target_pairs={{128,0},{136,8},{144,16},{152,24},{160,32},{168,40},{176,48},{184,... | collective-permute-start | bytes 792584 | tf_op jit(solution)/shard_map/ppermute | solution.py:15
  98.3 12.5 %collective-permute-start.12 = (f32[129,512]{1,0:T(8,128)S(1)}, f32[129,512]{1,0:T(8,128)S(1)}, u32[]{:S(2)}, u32[]{:S(2)}) collective-permute-start(f32[129,512]{1,0:T(8,128)S(1)} %pad_maximum_fusion.10), channel_id=1, source_target_pairs={{0,128},{8,136},{16,144},{24,152},{32,160},{40,168},{48,176},{56,1... | collective-permute-start | bytes 792584 | tf_op jit(solution)/shard_map/ppermute | solution.py:15
  109.4 19.8 %collective-permute-start.6 = (f32[129,512]{1,0:T(8,128)S(1)}, f32[129,512]{1,0:T(8,128)S(1)}, u32[]{:S(2)}, u32[]{:S(2)}) collective-permute-start(f32[129,512]{1,0:T(8,128)S(1)} %pad_maximum_fusion.6), channel_id=1, source_target_pairs={{256,0},{264,8},{272,16},{280,24},{288,32},{296,40},{304,48},{312,... | collective-permute-start | bytes 792584 | tf_op jit(solution)/shard_map/ppermute | solution.py:15
  110.8 23.9 %collective-permute-start.13 = (f32[129,512]{1,0:T(8,128)S(1)}, f32[129,512]{1,0:T(8,128)S(1)}, u32[]{:S(2)}, u32[]{:S(2)}) collective-permute-start(f32[129,512]{1,0:T(8,128)S(1)} %pad_maximum_fusion.11), channel_id=1, source_target_pairs={{0,256},{8,264},{16,272},{24,280},{32,288},{40,296},{48,304},{56,3... | collective-permute-start | bytes 792584 | tf_op jit(solution)/shard_map/ppermute | solution.py:15
Sparse Core Ops, SparseCore 0:
  136.9 86.3 all-reduce.2
where the time goes:
time: 235 us; the launch traced here: 233 us
  waiting for transfers between devices  119 us (51%)
  starting transfers between devices  57.6 us (25%)
  matrix products  27.7 us (12%)
  between operations  14.5 us (6%)
  other arithmetic  7.18 us (3%)
  local copies, waits for them, and re-layouts  7.07 us (3%)
    psum x1, waiting for transfers between devices, shards(): lax.psum(db_part.astype(jnp.bfloat16), 'head').astype(jnp.float32)  84.9 us
    ppermute x14, starting transfers between devices, shift(): return lax.ppermute(value, 'seq', pairs)  57.5 us
    ppermute x14, waiting for transfers between devices, shift(): return lax.ppermute(value, 'seq', pairs)  34 us
    dot_general x8, matrix products, head_step(): lax.dot_general(dy_head, x_head, (((1,), (1,)), ((), ())), preferred_elem...  11.2 us
    dot_general x8, matrix products, head_step(): lax.dot_general(mixing, dy_head, (((0,), (0,)), ((), ())), preferred_elem...  9.8 us
    unnamed x11, local copies, waits for them, and re-layouts  6.02 us
  transfers between devices with their start and end apart: 15, of which 10 were waited for; matrix products, arithmetic and copies ran while one was open for 13% of the time, Pallas kernels for 0%

commit v1 on v0

--- a/solution.py
+++ b/solution.py
@@ -98,7 +98,7 @@
         grad_out.astype(jnp.float32) * from_start_cols, state_in.T, precision=PRECISE
     )
     grad_b, grad_c = (
-        lax.psum(db_part.astype(jnp.bfloat16), "head").astype(jnp.float32),
+        jnp.sum(lax.all_gather(db_part.astype(jnp.bfloat16), "head"), axis=0).astype(jnp.float32),
         lax.psum(dc_part.astype(jnp.bfloat16), "head").astype(jnp.float32),
     )
     return (

time: 235 us -> 245 us (1.043)
  blocking collectives: 0 us -> 32.7 us
  waiting for transfers between devices: 119 us -> 105 us
  matrix products: 27.7 us -> 19.6 us
    all_gather x0 -> x1, blocking collectives: none -> 32.7 us  [shards(): lax.all_gather(db_part.astype(jnp.bfloat16), 'head')]
    psum x1, waiting for transfers between devices: 84.9 us -> 74.9 us  [shards(): lax.psum(dc_part.astype(jnp.bfloat16), 'head').astype(jnp.float32)]
    dot_general x8, matrix products: 9.8 us -> 2.7 us  [head_step(): lax.dot_general(mixing, dy_head, (((0,), (0,)), ((), ())), preferred_elem...]
    ppermute x14, waiting for transfers between devices: 34 us -> 30.5 us  [shift(): return lax.ppermute(value, 'seq', pairs)]
    unnamed x11 -> x10, local copies, waits for them, and re-layouts: 6.02 us -> 4.49 us
  transfers between devices with their start and end apart: 15 -> 15, of which waited for: 10 -> 9; matrix products, arithmetic and copies ran while one was open for 13% -> 9% of each run, Pallas kernels for 0% -> 0%
where the time goes in v1:
time: 245 us; the launch traced here: 244 us
  waiting for transfers between devices  105 us (43%)
  starting transfers between devices  57.6 us (24%)
  blocking collectives  32.7 us (13%)
  matrix products  19.6 us (8%)
  between operations  14.5 us (6%)
  other arithmetic  8.02 us (3%)
  local copies, waits for them, and re-layouts  5.53 us (2%)
    psum x1, waiting for transfers between devices, shards(): lax.psum(dc_part.astype(jnp.bfloat16), 'head').astype(jnp.float32)  74.9 us
    ppermute x14, starting transfers between devices, shift(): return lax.ppermute(value, 'seq', pairs)  57.5 us
    all_gather x1, blocking collectives, shards(): lax.all_gather(db_part.astype(jnp.bfloat16), 'head')  32.7 us
    ppermute x14, waiting for transfers between devices, shift(): return lax.ppermute(value, 'seq', pairs)  30.5 us
    dot_general x8, matrix products, head_step(): lax.dot_general(dy_head, x_head, (((1,), (1,)), ((), ())), preferred_elem...  10.8 us
  transfers between devices with their start and end apart: 15, of which 9 were waited for; matrix products, arithmetic and copies ran while one was open for 9% of the time, Pallas kernels for 0%

profile of v1, /device:TPU:2, one launch (start us, length us, event | category | flops | bytes accessed | tf_op | source)
XLA Modules:
  0.0 243.7 jit_solution(2287746485624188373)
XLA Ops:
  7.2 1.9 reduce-window.6
  9.2 0.2 slice_reduce_fusion
  9.4 0.2 slice_reduce_fusion.1
  9.8 1.2 copy.15
  11.1 0.6 fusion.21
  11.9 0.2 copy-done.2
  12.1 0.2 copy.13
  12.3 0.3 copy-done.1
  12.7 0.6 fusion.20
  13.5 0.9 pad_maximum_fusion
  14.3 1.9 collective-permute-start
  16.2 2.4 collective-permute-start.7
  18.7 0.3 fusion.47
  19.0 14.0 %while.17 = (s32[]{:T(128)}, f32[384,384]{1,0:T(8,128)S(1)}, f32[384,512]{0,1:T(8,128)S(1)}, f32[8,384]{1,0:T(8,128)S(1)}, bf16[384,512]{1,0:T(8,128)(2,1)S(1)},...) while((s32[]{:T(128)}, f32[384,384]{1,0:T(8,128)S(1)}, ...), condition=%wide.region_3.4_spmd.clone.clone, body=%wide.region_2.3_spmd.clone.clone.sunk | while | flops 39665672 | bytes 2176688 | solution.py:85
  19.0 1.3 fusion.64
  20.4 0.3 convolution_dynamic-update-slice_fusion.2
  20.8 1.3 fusion.64
  22.1 0.3 convolution_dynamic-update-slice_fusion.2
  22.5 1.3 fusion.64
  23.9 0.3 convolution_dynamic-update-slice_fusion.2
  24.3 1.3 fusion.64
  25.6 0.3 convolution_dynamic-update-slice_fusion.2
  26.0 1.3 fusion.64
  27.4 0.3 convolution_dynamic-update-slice_fusion.2
  27.8 1.3 fusion.64
  29.1 0.3 convolution_dynamic-update-slice_fusion.2
  29.5 1.3 fusion.64
  30.9 0.3 convolution_dynamic-update-slice_fusion.2
  31.2 1.3 fusion.64
  32.6 0.3 convolution_dynamic-update-slice_fusion.2
  33.0 7.4 %collective-permute-start.1 = (f32[129,512]{1,0:T(8,128)}, f32[129,512]{1,0:T(8,128)S(1)}, u32[]{:S(2)}, u32[]{:S(2)}) collective-permute-start(f32[129,512]{1,0:T(8,128)} %collective-permute-done), channel_id=1, source_target_pairs={{8,0},{16,8},{24,16},{32,24},{40,32},{48,40},{56,48},{64,56},{72,6... | collective-permute-start | bytes 792584 | tf_op jit(solution)/shard_map/ppermute | solution.py:15
  40.4 0.3 fusion.41
  40.8 0.2 fusion.39
  41.1 1.9 collective-permute-start.8
  43.0 1.8 collective-permute-done.1
  44.8 0.7 slice_multiply_fusion.21
  45.5 1.0 fusion.38
  46.5 1.9 collective-permute-start.2
  48.5 0.7 collective-permute-done.8
  49.2 0.7 slice_multiply_fusion.16
  49.9 1.0 fusion.32
  50.9 3.2 %collective-permute-start.9 = (f32[129,512]{1,0:T(8,128)S(1)}, f32[129,512]{1,0:T(8,128)S(1)}, u32[]{:S(2)}, u32[]{:S(2)}) collective-permute-start(f32[129,512]{1,0:T(8,128)S(1)} %pad_maximum_fusion.7), channel_id=1, source_target_pairs={{0,16},{8,24},{16,32},{24,40},{32,48},{40,56},{48,64},{56,72},{64,... | collective-permute-start | bytes 792584 | tf_op jit(solution)/shard_map/ppermute | solution.py:15
  54.2 0.8 collective-permute-done.2
  55.1 1.3 collective-permute-start.3
  56.4 11.7 %collective-permute-done.9 = f32[129,512]{1,0:T(8,128)S(1)} collective-permute-done((f32[129,512]{1,0:T(8,128)S(1)}, f32[129,512]{1,0:T(8,128)S(1)}, u32[]{:S(2)}, u32[]{:S(2)}) %collective-permute-start.9) | collective-permute-done | bytes 264224 | tf_op jit(solution)/shard_map/ppermute | solution.py:15
  68.2 2.3 collective-permute-start.10
  70.6 1.3 collective-permute-start.4
  71.9 5.3 %collective-permute-done.10 = f32[129,512]{1,0:T(8,128)S(1)} collective-permute-done((f32[129,512]{1,0:T(8,128)S(1)}, f32[129,512]{1,0:T(8,128)S(1)}, u32[]{:S(2)}, u32[]{:S(2)}) %collective-permute-start.10) | collective-permute-done | bytes 264224 | tf_op jit(solution)/shard_map/ppermute | solution.py:15
  77.3 7.9 %collective-permute-start.11 = (f32[129,512]{1,0:T(8,128)S(1)}, f32[129,512]{1,0:T(8,128)S(1)}, u32[]{:S(2)}, u32[]{:S(2)}) collective-permute-start(f32[129,512]{1,0:T(8,128)S(1)} %pad_maximum_fusion.9), channel_id=1, source_target_pairs={{0,64},{8,72},{16,80},{24,88},{32,96},{40,104},{48,112},{56,120},{... | collective-permute-start | bytes 792584 | tf_op jit(solution)/shard_map/ppermute | solution.py:15
  85.3 1.3 collective-permute-start.5
  86.6 4.1 %collective-permute-done.11 = f32[129,512]{1,0:T(8,128)S(1)} collective-permute-done((f32[129,512]{1,0:T(8,128)S(1)}, f32[129,512]{1,0:T(8,128)S(1)}, u32[]{:S(2)}, u32[]{:S(2)}) %collective-permute-start.11) | collective-permute-done | bytes 264224 | tf_op jit(solution)/shard_map/ppermute | solution.py:15
  90.9 5.4 %collective-permute-start.12 = (f32[129,512]{1,0:T(8,128)S(1)}, f32[129,512]{1,0:T(8,128)S(1)}, u32[]{:S(2)}, u32[]{:S(2)}) collective-permute-start(f32[129,512]{1,0:T(8,128)S(1)} %pad_maximum_fusion.10), channel_id=1, source_target_pairs={{0,128},{8,136},{16,144},{24,152},{32,160},{40,168},{48,176},{56,1... | collective-permute-start | bytes 792584 | tf_op jit(solution)/shard_map/ppermute | solution.py:15
  96.3 5.6 %collective-permute-done.5 = f32[129,512]{1,0:T(8,128)S(1)} collective-permute-done((f32[129,512]{1,0:T(8,128)S(1)}, f32[129,512]{1,0:T(8,128)S(1)}, u32[]{:S(2)}, u32[]{:S(2)}) %collective-permute-start.5) | collective-permute-done | bytes 264224 | tf_op jit(solution)/shard_map/ppermute | solution.py:15
  102.0 1.3 collective-permute-start.6
  103.4 17.8 %collective-permute-start.13 = (f32[129,512]{1,0:T(8,128)S(1)}, f32[129,512]{1,0:T(8,128)S(1)}, u32[]{:S(2)}, u32[]{:S(2)}) collective-permute-start(f32[129,512]{1,0:T(8,128)S(1)} %pad_maximum_fusion.11), channel_id=1, source_target_pairs={{0,256},{8,264},{16,272},{24,280},{32,288},{40,296},{48,304},{56,3... | collective-permute-start | bytes 792584 | tf_op jit(solution)/shard_map/ppermute | solution.py:15
  121.3 0.6 collective-permute-done.6
  121.8 1.4 fusion.18
  123.2 32.7 %all-gather = bf16[3072,128]{1,0:T(8,128)(2,1)S(1)} all-gather(bf16[384,128]{1,0:T(8,128)(2,1)S(1)} %fusion.18), channel_id=2, replica_groups=mesh['seq'=64,'head'=8] {'head'}, dimensions={0}, use_global_device_ids=true | all-gather | bytes 884736 | tf_op jit(solution)/shard_map/all_gather | solution.py:101
  155.9 2.0 fusion.19
  158.0 0.7 fusion.17
  158.7 0.9 copy.19
  159.7 0.8 reduce_sum.12
  160.4 74.9 %all-reduce.2.cloned.1.call-done = bf16[384,128]{1,0:T(8,128)(2,1)} async-done(((bf16[384,128]{1,0:T(8,128)(2,1)}), bf16[384,128]{1,0:T(8,128)(2,1)}) %all-reduce.2.cloned.1.call-update) | async-done | bytes 98320 | tf_op jit(solution)/shard_map/psum | solution.py:102
  235.3 1.5 copy.31
  (61 shorter events, 1.8 us)
Async XLA Ops:
  7.2 3.9 %copy-start = (bf16[384,128]{1,0:T(8,128)(2,1)S(1)}, bf16[384,128]{1,0:T(8,128)(2,1)}, u32[]{:S(2)}) copy-start(bf16[384,128]{1,0:T(8,128)(2,1)} %param.8) | copy-start | bytes 294916
  7.2 228.1 %all-reduce.2.cloned.1.call-start = ((), (), s32[]{:S(2)}) async-start(), calls=%async_computation | async-start | bytes 196608 | tf_op jit(solution)/shard_map/psum | solution.py:102
  11.1 1.0 copy-start.2
  11.8 0.9 copy-start.1
  14.3 18.6 %collective-permute-start = (f32[129,512]{1,0:T(8,128)}, f32[129,512]{1,0:T(8,128)}, u32[]{:S(2)}, u32[]{:S(2)}) collective-permute-start(f32[129,512]{1,0:T(8,128)} %get-tuple-element.223), channel_id=1, source_target_pairs={{8,0},{16,8},{24,16},{32,24},{40,32},{48,40},{56,48},{64,56},{72,6... | collective-permute-start | bytes 792584 | tf_op jit(solution)/shard_map/ppermute | solution.py:15
  16.2 24.8 %collective-permute-start.7 = (f32[129,512]{1,0:T(8,128)}, f32[129,512]{1,0:T(8,128)}, u32[]{:S(2)}, u32[]{:S(2)}) collective-permute-start(f32[129,512]{1,0:T(8,128)} %get-tuple-element.222), channel_id=1, source_target_pairs={{0,8},{8,16},{16,24},{24,32},{32,40},{40,48},{48,56},{56,64},{64,7... | collective-permute-start | bytes 792584 | tf_op jit(solution)/shard_map/ppermute | solution.py:15
  33.0 11.8 %collective-permute-start.1 = (f32[129,512]{1,0:T(8,128)}, f32[129,512]{1,0:T(8,128)S(1)}, u32[]{:S(2)}, u32[]{:S(2)}) collective-permute-start(f32[129,512]{1,0:T(8,128)} %collective-permute-done), channel_id=1, source_target_pairs={{8,0},{16,8},{24,16},{32,24},{40,32},{48,40},{56,48},{64,56},{72,6... | collective-permute-start | bytes 792584 | tf_op jit(solution)/shard_map/ppermute | solution.py:15
  41.1 8.1 %collective-permute-start.8 = (f32[129,512]{1,0:T(8,128)}, f32[129,512]{1,0:T(8,128)S(1)}, u32[]{:S(2)}, u32[]{:S(2)}) collective-permute-start(f32[129,512]{1,0:T(8,128)} %collective-permute-done.7), channel_id=1, source_target_pairs={{0,8},{8,16},{16,24},{24,32},{32,40},{40,48},{48,56},{56,64},{64,7... | collective-permute-start | bytes 792584 | tf_op jit(solution)/shard_map/ppermute | solution.py:15
  46.5 8.4 %collective-permute-start.2 = (f32[129,512]{1,0:T(8,128)S(1)}, f32[129,512]{1,0:T(8,128)S(1)}, u32[]{:S(2)}, u32[]{:S(2)}) collective-permute-start(f32[129,512]{1,0:T(8,128)S(1)} %pad_maximum_fusion.2), channel_id=1, source_target_pairs={{16,0},{24,8},{32,16},{40,24},{48,32},{56,40},{64,48},{72,56},{80,... | collective-permute-start | bytes 792584 | tf_op jit(solution)/shard_map/ppermute | solution.py:15
  50.9 17.1 %collective-permute-start.9 = (f32[129,512]{1,0:T(8,128)S(1)}, f32[129,512]{1,0:T(8,128)S(1)}, u32[]{:S(2)}, u32[]{:S(2)}) collective-permute-start(f32[129,512]{1,0:T(8,128)S(1)} %pad_maximum_fusion.7), channel_id=1, source_target_pairs={{0,16},{8,24},{16,32},{24,40},{32,48},{40,56},{48,64},{56,72},{64,... | collective-permute-start | bytes 792584 | tf_op jit(solution)/shard_map/ppermute | solution.py:15
  55.1 15.4 %collective-permute-start.3 = (f32[129,512]{1,0:T(8,128)S(1)}, f32[129,512]{1,0:T(8,128)S(1)}, u32[]{:S(2)}, u32[]{:S(2)}) collective-permute-start(f32[129,512]{1,0:T(8,128)S(1)} %pad_maximum_fusion.3), channel_id=1, source_target_pairs={{32,0},{40,8},{48,16},{56,24},{64,32},{72,40},{80,48},{88,56},{96,... | collective-permute-start | bytes 792584 | tf_op jit(solution)/shard_map/ppermute | solution.py:15
  68.2 9.0 %collective-permute-start.10 = (f32[129,512]{1,0:T(8,128)S(1)}, f32[129,512]{1,0:T(8,128)S(1)}, u32[]{:S(2)}, u32[]{:S(2)}) collective-permute-start(f32[129,512]{1,0:T(8,128)S(1)} %pad_maximum_fusion.8), channel_id=1, source_target_pairs={{0,32},{8,40},{16,48},{24,56},{32,64},{40,72},{48,80},{56,88},{64,... | collective-permute-start | bytes 792584 | tf_op jit(solution)/shard_map/ppermute | solution.py:15
  70.6 14.6 %collective-permute-start.4 = (f32[129,512]{1,0:T(8,128)S(1)}, f32[129,512]{1,0:T(8,128)S(1)}, u32[]{:S(2)}, u32[]{:S(2)}) collective-permute-start(f32[129,512]{1,0:T(8,128)S(1)} %pad_maximum_fusion.4), channel_id=1, source_target_pairs={{64,0},{72,8},{80,16},{88,24},{96,32},{104,40},{112,48},{120,56},{... | collective-permute-start | bytes 792584 | tf_op jit(solution)/shard_map/ppermute | solution.py:15
  77.3 13.5 %collective-permute-start.11 = (f32[129,512]{1,0:T(8,128)S(1)}, f32[129,512]{1,0:T(8,128)S(1)}, u32[]{:S(2)}, u32[]{:S(2)}) collective-permute-start(f32[129,512]{1,0:T(8,128)S(1)} %pad_maximum_fusion.9), channel_id=1, source_target_pairs={{0,64},{8,72},{16,80},{24,88},{32,96},{40,104},{48,112},{56,120},{... | collective-permute-start | bytes 792584 | tf_op jit(solution)/shard_map/ppermute | solution.py:15
  85.3 16.6 %collective-permute-start.5 = (f32[129,512]{1,0:T(8,128)S(1)}, f32[129,512]{1,0:T(8,128)S(1)}, u32[]{:S(2)}, u32[]{:S(2)}) collective-permute-start(f32[129,512]{1,0:T(8,128)S(1)} %pad_maximum_fusion.5), channel_id=1, source_target_pairs={{128,0},{136,8},{144,16},{152,24},{160,32},{168,40},{176,48},{184,... | collective-permute-start | bytes 792584 | tf_op jit(solution)/shard_map/ppermute | solution.py:15
  90.9 12.5 %collective-permute-start.12 = (f32[129,512]{1,0:T(8,128)S(1)}, f32[129,512]{1,0:T(8,128)S(1)}, u32[]{:S(2)}, u32[]{:S(2)}) collective-permute-start(f32[129,512]{1,0:T(8,128)S(1)} %pad_maximum_fusion.10), channel_id=1, source_target_pairs={{0,128},{8,136},{16,144},{24,152},{32,160},{40,168},{48,176},{56,1... | collective-permute-start | bytes 792584 | tf_op jit(solution)/shard_map/ppermute | solution.py:15
  102.0 19.8 %collective-permute-start.6 = (f32[129,512]{1,0:T(8,128)S(1)}, f32[129,512]{1,0:T(8,128)S(1)}, u32[]{:S(2)}, u32[]{:S(2)}) collective-permute-start(f32[129,512]{1,0:T(8,128)S(1)} %pad_maximum_fusion.6), channel_id=1, source_target_pairs={{256,0},{264,8},{272,16},{280,24},{288,32},{296,40},{304,48},{312,... | collective-permute-start | bytes 792584 | tf_op jit(solution)/shard_map/ppermute | solution.py:15
  103.4 52.5 %collective-permute-start.13 = (f32[129,512]{1,0:T(8,128)S(1)}, f32[129,512]{1,0:T(8,128)S(1)}, u32[]{:S(2)}, u32[]{:S(2)}) collective-permute-start(f32[129,512]{1,0:T(8,128)S(1)} %pad_maximum_fusion.11), channel_id=1, source_target_pairs={{0,256},{8,264},{16,272},{24,280},{32,288},{40,296},{48,304},{56,3... | collective-permute-start | bytes 792584 | tf_op jit(solution)/shard_map/ppermute | solution.py:15
Sparse Core Ops, SparseCore 0:
  158.1 77.1 all-reduce.1
